TPU v7x, 32 devices: a whole 2x2x4 slice. The times are simulated.
32 devices in a mesh: snap: 2 (over y), chan: 16 (over z, x, core).
Axes of the slice: x: 2, y: 2, z: 4, core: 2. Of those that a mesh axis runs over, the one named last changes fastest.
Arguments:
- snap_tiles: bfloat16 [16, 192, 64, 128], P('snap', 'chan'), may hold values from -6 to 6
- beam_gain: float32 [16, 64, 128], P('snap'), may hold values from 0.1 to 1
- kernel: bfloat16 [16, 32, 128, 256], P(None, 'snap'), may hold values from -0.5 to 0.5
- tile_map: int32 [16, 32], replicated, may hold values from 0 to 63
- pixel_lm: float32 [2, 8192], P(None, 'snap'), may hold values from -0.5 to 0.5
- mode_uv: int32 [2, 2048], replicated, may hold values from -32 to 31
Outputs:
- sky_cube: float32 [32, 192, 256], P('snap', 'chan')
- delay_spec: float32 [2, 192, 2048], P(None, None, ('snap', 'chan'))
Inputs may be any that keep to these rules, and one draw needn't show every extreme that they name: `tile_map`: tile indices.
All inputs are finite; a program needn't handle non-finite values.
Results may differ from a plain program's by a relative error of at most 0.0047.
Values may be sent and summed in bfloat16 or wider, within the bound.
No kernel may reach another device: no remote copies, remote signals or barrier semaphores. Data moves between devices by JAX's collectives and lax.ppermute only.
A program may use at most 192 MiB of HBM per device.

v0:
```python
import math
import jax
import jax.numpy as jnp
from jax import lax
from jax.sharding import PartitionSpec as P

BLOCK_PIX = 256


def hamming(length):
    channel_index = jnp.arange(length, dtype=jnp.float32)
    return 0.54 - 0.46 * jnp.cos(channel_index * (2.0 * math.pi / (length - 1)))


def delay_transform(power_spectrum):
    length = power_spectrum.shape[1]
    channel_index = jnp.arange(length, dtype=jnp.int32)
    residues = channel_index[:, None] * channel_index[None, :] % length
    phases = residues.astype(jnp.float32) * (2.0 * math.pi / length)
    cosine = jnp.cos(phases)
    sine_part = jnp.sin(phases)
    window_gain = hamming(length)[:, None]
    real_component = power_spectrum[0] * window_gain
    imag_part = power_spectrum[1] * window_gain
    highest = lax.Precision.HIGHEST
    out_re = jnp.dot(cosine, real_component, precision=highest) + jnp.dot(
        sine_part, imag_part, precision=highest
    )
    out_im = jnp.dot(cosine, imag_part, precision=highest) - jnp.dot(
        sine_part, real_component, precision=highest
    )
    return jnp.stack([out_re, out_im]) / math.sqrt(length)


def phasor(positions, uv_grid):
    spatial = uv_grid.astype(jnp.float32)
    phase_table = (
        positions[0][:, None] * spatial[0][None, :] + positions[1][:, None] * spatial[1][None, :]
    ) * (2.0 * math.pi)
    return jnp.concatenate([jnp.cos(phase_table), -jnp.sin(phase_table)], axis=1).astype(
        jnp.bfloat16
    )


def interpolate(weighted, kernels, block_maps):
    gathered_rows = jax.vmap(
        lambda single_snapshot_tiles, one_map: jnp.take(single_snapshot_tiles, one_map, axis=1)
    )(weighted, block_maps)
    return jnp.einsum("scbt,sbtp->bcp", gathered_rows, kernels, preferred_element_type=jnp.float32)


def per_device(snap_tiles, beam_gain, kernel, tile_map, pixel_lm, mode_uv):
    snap_count = lax.axis_size("snap")
    chan_count = lax.axis_size("chan")
    snap_index = lax.axis_index("snap")
    chan_local = snap_tiles.shape[1]
    local_pixel_blocks = pixel_lm.shape[1] // BLOCK_PIX
    block_start = snap_index * local_pixel_blocks
    weighted = (snap_tiles.astype(jnp.float32) * beam_gain[:, None]).astype(jnp.bfloat16)
    own_map = lax.dynamic_slice_in_dim(tile_map, block_start, local_pixel_blocks, 1)
    sky_cube = interpolate(lax.all_gather(weighted, "snap", axis=0, tiled=True), kernel, own_map)
    cube_low = sky_cube.astype(jnp.bfloat16)
    per_group = 2
    turn_count = local_pixel_blocks // per_group
    group_width = per_group * BLOCK_PIX
    fourier_mode_count = mode_uv.shape[1]

    def add_group(turn, running):
        partial_sky_cube = lax.dynamic_slice_in_dim(cube_low, turn * per_group, per_group, 0)
        lm_part = lax.dynamic_slice_in_dim(pixel_lm, turn * group_width, group_width, 1)
        phasor_lookup = phasor(lm_part, mode_uv).reshape(
            per_group, BLOCK_PIX, 2 * fourier_mode_count
        )
        return running + jnp.einsum(
            "woj,wjh->oh", partial_sky_cube, phasor_lookup, preferred_element_type=jnp.float32
        )

    running = lax.fori_loop(
        0, turn_count, add_group, jnp.zeros((chan_local, 2 * fourier_mode_count), jnp.float32)
    )
    partial_value = running.reshape(chan_local, 2, fourier_mode_count).transpose(1, 0, 2)
    pixel_total = pixel_lm.shape[1] * snap_count
    cell_count = fourier_mode_count // (snap_count * chan_count)
    spread = partial_value.reshape(2, chan_local, snap_count, chan_count, cell_count)
    regrouped = lax.all_to_all(spread, "chan", split_axis=3, concat_axis=1, tiled=True)
    summed = lax.psum_scatter(regrouped, "snap", scatter_dimension=2, tiled=True)
    scaled = summed.reshape(2, chan_local * chan_count, cell_count) / math.sqrt(pixel_total)
    delay_spec = delay_transform(scaled)
    return (sky_cube, delay_spec)


def solution(mesh):
    return jax.shard_map(
        per_device,
        mesh=mesh,
        in_specs=(
            P("snap", "chan", None, None),
            P("snap", None, None),
            P(None, "snap", None, None),
            P(),
            P(None, "snap"),
            P(),
        ),
        out_specs=(P("snap", "chan", None), P(None, None, ("snap", "chan"))),
        check_vma=False,
    )
```

profile of v0, /device:TPU:0, one launch (start us, length us, event | category | flops | bytes accessed | tf_op | source)
XLA Modules:
  0.0 277.3 jit_solution(12588027699825546951)
XLA Ops:
  7.2 3.1 %multiply_convert_fusion = bf16[8,12,64,128]{3,2,1,0:T(8,128)(2,1)} fusion(bf16[8,12,64,128]{3,2,1,0:T(8,128)(2,1)} %param.8, f32[8,64,128]{2,1,0:T(8,128)} %param.9), kind=kLoop, calls=%fused_computation.16 | loop fusion | flops 2359296 | bytes 3407872 | tf_op jit(solution)/shard_map/convert_element_type | solution.py:59
  10.7 0.1 copy.26
  10.8 47.4 %all-gather.2.cloned.1.call-done = bf16[16,12,64,128]{3,2,1,0:T(8,128)(2,1)} async-done(((bf16[8,12,64,128]{3,2,1,0:T(8,128)(2,1)}), bf16[16,12,64,128]{3,2,1,0:T(8,128)(2,1)}) %all-gather.2.cloned.1.call-update) | async-done | bytes 3145744 | tf_op jit(solution)/shard_map/all_gather | solution.py:61
  58.2 6.5 %copy.27 = bf16[16,12,64,128]{3,1,2,0:T(8,128)(2,1)} copy(bf16[16,12,64,128]{3,2,1,0:T(8,128)(2,1)} %all-gather.2.cloned.1.call-done) | data formatting | bytes 6291456 | tf_op jit(solution)/shard_map/all_gather | solution.py:61
  64.6 3.4 %gather_fusion = bf16[256,12,128]{2,1,0:T(8,128)(2,1)S(1)} fusion(bf16[16,12,64,128]{3,1,2,0:T(8,128)(2,1)} %copy.27, s32[256]{0:T(256)S(1)} %reshape.93), kind=kCustom, calls=%fused_computation | custom fusion | bytes 1574912 | tf_op jit(solution)/shard_map/vmap(jit(_take))/gather | solution.py:47
  68.1 7.0 %fusion.67 = (bf16[16,12,256]{2,1,0:T(8,128)(2,1)S(1)}, f32[16,12,256]{2,1,0:T(8,128)S(1)}) fusion(bf16[16,16,128,256]{3,2,1,0:T(8,128)(2,1)} %param.10, bf16[16,16,12,128]{3,2,1,0:T(8,128)(2,1)S(1)} %bitcast.60, pred[16,16]{0,1:T(8,128)(4,1)S(1)} %copy.26), kind=kOutput, calls=%fused_computation.74 | convolution fusion | flops 201768960 | bytes 17858816 | tf_op jit(solution)/shard_map/scbt,sbtp->bcp/dot_general | solution.py:49
  75.1 162.2 %while.16 = (s32[]{:T(128)}, f32[12,4096]{1,0:T(8,128)S(1)}, bf16[16,12,256]{2,1,0:T(8,128)(2,1)S(1)}, f32[2,4096]{1,0:T(2,128)}, f32[2,2048]{1,0:T(2,128)S(1)},...) while((s32[]{:T(128)}, f32[12,4096]{1,0:T(8,128)S(1)}, ...), condition=%wide.region_1.2_spmd.clone, body=%wide.region_0.1_spmd.clone.sunk | while | flops 66158604 | bytes 8933627 | solution.py:78
  75.1 0.9 dynamic-slice_reduce_fusion.3
  76.0 17.1 %cosine_convert_fusion.2 = (bf16[2,256,2048]{2,1,0:T(8,128)(2,1)S(1)}, bf16[2,256,2048]{2,1,0:T(8,128)(2,1)}) fusion(f32[2048]{0:T(1024)S(1)} %bitcast.58, f32[2,256]{1,0:T(2,128)S(1)} %mul.440, f32[2048]{0:T(1024)S(1)} %bitcast.57, f32[2,256]{1,0:T(2,128)S(1)} %mul.441), kind=kLoop, calls=%fused_computation.7.clone.1 | loop fusion | flops 7340032 | bytes 4214784 | tf_op jit(solution)/shard_map/convert
  93.1 2.2 fusion.75
  95.4 0.9 dynamic-slice_reduce_fusion.3
  96.3 17.1 %cosine_convert_fusion.2 = (bf16[2,256,2048]{2,1,0:T(8,128)(2,1)S(1)}, bf16[2,256,2048]{2,1,0:T(8,128)(2,1)}) fusion(f32[2048]{0:T(1024)S(1)} %bitcast.58, f32[2,256]{1,0:T(2,128)S(1)} %mul.440, f32[2048]{0:T(1024)S(1)} %bitcast.57, f32[2,256]{1,0:T(2,128)S(1)} %mul.441), kind=kLoop, calls=%fused_computation.7.clone.1 | loop fusion | flops 7340032 | bytes 4214784 | tf_op jit(solution)/shard_map/convert
  113.4 2.2 fusion.75
  115.7 0.9 dynamic-slice_reduce_fusion.3
  116.5 17.1 %cosine_convert_fusion.2 = (bf16[2,256,2048]{2,1,0:T(8,128)(2,1)S(1)}, bf16[2,256,2048]{2,1,0:T(8,128)(2,1)}) fusion(f32[2048]{0:T(1024)S(1)} %bitcast.58, f32[2,256]{1,0:T(2,128)S(1)} %mul.440, f32[2048]{0:T(1024)S(1)} %bitcast.57, f32[2,256]{1,0:T(2,128)S(1)} %mul.441), kind=kLoop, calls=%fused_computation.7.clone.1 | loop fusion | flops 7340032 | bytes 4214784 | tf_op jit(solution)/shard_map/convert
  133.6 2.2 fusion.75
  135.9 0.9 dynamic-slice_reduce_fusion.3
  136.8 17.1 %cosine_convert_fusion.2 = (bf16[2,256,2048]{2,1,0:T(8,128)(2,1)S(1)}, bf16[2,256,2048]{2,1,0:T(8,128)(2,1)}) fusion(f32[2048]{0:T(1024)S(1)} %bitcast.58, f32[2,256]{1,0:T(2,128)S(1)} %mul.440, f32[2048]{0:T(1024)S(1)} %bitcast.57, f32[2,256]{1,0:T(2,128)S(1)} %mul.441), kind=kLoop, calls=%fused_computation.7.clone.1 | loop fusion | flops 7340032 | bytes 4214784 | tf_op jit(solution)/shard_map/convert
  153.9 2.2 fusion.75
  156.2 0.9 dynamic-slice_reduce_fusion.3
  157.1 17.1 %cosine_convert_fusion.2 = (bf16[2,256,2048]{2,1,0:T(8,128)(2,1)S(1)}, bf16[2,256,2048]{2,1,0:T(8,128)(2,1)}) fusion(f32[2048]{0:T(1024)S(1)} %bitcast.58, f32[2,256]{1,0:T(2,128)S(1)} %mul.440, f32[2048]{0:T(1024)S(1)} %bitcast.57, f32[2,256]{1,0:T(2,128)S(1)} %mul.441), kind=kLoop, calls=%fused_computation.7.clone.1 | loop fusion | flops 7340032 | bytes 4214784 | tf_op jit(solution)/shard_map/convert
  174.2 2.2 fusion.75
  176.5 0.9 dynamic-slice_reduce_fusion.3
  177.4 17.1 %cosine_convert_fusion.2 = (bf16[2,256,2048]{2,1,0:T(8,128)(2,1)S(1)}, bf16[2,256,2048]{2,1,0:T(8,128)(2,1)}) fusion(f32[2048]{0:T(1024)S(1)} %bitcast.58, f32[2,256]{1,0:T(2,128)S(1)} %mul.440, f32[2048]{0:T(1024)S(1)} %bitcast.57, f32[2,256]{1,0:T(2,128)S(1)} %mul.441), kind=kLoop, calls=%fused_computation.7.clone.1 | loop fusion | flops 7340032 | bytes 4214784 | tf_op jit(solution)/shard_map/convert
  194.5 2.2 fusion.75
  196.7 0.9 dynamic-slice_reduce_fusion.3
  197.6 17.1 %cosine_convert_fusion.2 = (bf16[2,256,2048]{2,1,0:T(8,128)(2,1)S(1)}, bf16[2,256,2048]{2,1,0:T(8,128)(2,1)}) fusion(f32[2048]{0:T(1024)S(1)} %bitcast.58, f32[2,256]{1,0:T(2,128)S(1)} %mul.440, f32[2048]{0:T(1024)S(1)} %bitcast.57, f32[2,256]{1,0:T(2,128)S(1)} %mul.441), kind=kLoop, calls=%fused_computation.7.clone.1 | loop fusion | flops 7340032 | bytes 4214784 | tf_op jit(solution)/shard_map/convert
  214.7 2.2 fusion.75
  217.0 0.9 dynamic-slice_reduce_fusion.3
  217.9 17.1 %cosine_convert_fusion.2 = (bf16[2,256,2048]{2,1,0:T(8,128)(2,1)S(1)}, bf16[2,256,2048]{2,1,0:T(8,128)(2,1)}) fusion(f32[2048]{0:T(1024)S(1)} %bitcast.58, f32[2,256]{1,0:T(2,128)S(1)} %mul.440, f32[2048]{0:T(1024)S(1)} %bitcast.57, f32[2,256]{1,0:T(2,128)S(1)} %mul.441), kind=kLoop, calls=%fused_computation.7.clone.1 | loop fusion | flops 7340032 | bytes 4214784 | tf_op jit(solution)/shard_map/convert
  235.0 2.2 fusion.75
  237.2 0.2 reshape.91
  237.4 0.3 reshape.92
  237.7 0.2 copy.51
  237.9 0.4 reshape.118
  238.3 14.4 %all_to_all.18 = f32[16,1,3072]{2,1,0:T(1,128)S(1)} all-to-all(f32[16,1,3072]{2,1,0:T(1,128)S(1)} %reshape.118), channel_id=1, replica_groups=mesh['snap'=2,'chan'=16] {'chan'}, dimensions={0} | all-to-all | bytes 393216 | tf_op jit(solution)/shard_map/all_to_all | solution.py:85
  252.7 0.5 broadcast.118
  253.2 1.1 reduce.8
  254.3 0.3 reshape.119
  254.6 1.0 copy.32
  255.7 0.8 copy.34
  256.5 8.1 %reduce-scatter.2.cloned.1.call-done = f32[2,192,1,1,64]{1,4,3,0,2:T(8,128)} async-done(((f32[2,192,2,1,64]{1,4,3,0,2:T(8,128)}), f32[2,192,1,1,64]{1,4,3,0,2:T(8,128)}) %reduce-scatter.2.cloned.1.call-update) | async-done | bytes 98320 | tf_op jit(solution)/shard_map/reduce_scatter | solution.py:86
  264.5 0.9 fusion.65
  265.5 1.1 fusion.23
  266.5 1.1 fusion.25
  267.6 1.1 fusion.12
  268.7 1.1 fusion.13
  269.8 0.7 maximum_multiply_fusion
  (38 shorter events, 0.8 us)
Async XLA Ops:
  7.2 3.3 %copy-start = (s32[16,32]{1,0:T(8,128)S(1)}, s32[16,32]{1,0:T(8,128)}, u32[]{:S(2)}) copy-start(s32[16,32]{1,0:T(8,128)} %param.11) | copy-start | bytes 6148
  7.2 3.6 %copy-start.1 = (s32[2,2048]{1,0:T(2,128)S(1)}, s32[2,2048]{1,0:T(2,128)}, u32[]{:S(2)}) copy-start(s32[2,2048]{1,0:T(2,128)} %param.13) | copy-start | bytes 49156
  7.2 51.0 %all-gather.2.cloned.1.call-start = ((), (), s32[]{:S(2)}) async-start(), calls=%async_computation.2 | async-start | bytes 4718592 | tf_op jit(solution)/shard_map/all_gather | solution.py:61
  10.4 254.1 %reduce-scatter.2.cloned.1.call-start = ((), (), s32[]{:S(2)}) async-start(), calls=%async_computation.3 | async-start | bytes 393216 | tf_op jit(solution)/shard_map/reduce_scatter | solution.py:86
Sparse Core Ops, SparseCore 0:
  10.5 47.6 all-gather.1
  255.7 8.7 reduce-scatter.1
where the time goes:
time: 278 us; the launch traced here: 277 us
  other arithmetic  143 us (51%)
  waiting for transfers between devices  55.4 us (20%)
  matrix products  29.4 us (11%)
  local copies, waits for them, and re-layouts  20.9 us (8%)
  blocking collectives  14.4 us (5%)
  between operations  14.1 us (5%)
    another operation x8, other arithmetic  137 us
    all_gather x1, waiting for transfers between devices, per_device(): lax.all_gather(weighted, 'snap', axis=0, tiled=True)  47.4 us
    dot_general x8, matrix products, add_group(): jnp.einsum('woj,wjh->oh', partial_sky_cube, phasor_lookup, preferred_elem...  18 us
    all_to_all x1, blocking collectives, per_device(): lax.all_to_all(spread, 'chan', split_axis=3, concat_axis=1, tiled=True)  14.4 us
    reduce_scatter x1, waiting for transfers between devices, per_device(): lax.psum_scatter(regrouped, 'snap', scatter_dimension=2, tiled=True)  8.05 us
    dot_general x1, matrix products, interpolate(): jnp.einsum('scbt,sbtp->bcp', gathered_rows, kernels, preferred_element_ty...  7.02 us
    slice x8, local copies, waits for them, and re-layouts, phasor(): positions[0][:, None] * spatial[0][None, :]  6.85 us
    all_gather x1, local copies, waits for them, and re-layouts, per_device(): lax.all_gather(weighted, 'snap', axis=0, tiled=True)  6.46 us
  transfers between devices with their start and end apart: 2, of which 2 were waited for; matrix products, arithmetic and copies ran while one was open for 0% of the time, Pallas kernels for 0%

commit v1 on v0

--- a/solution.py
+++ b/solution.py
@@ -5,6 +5,18 @@
 from jax.sharding import PartitionSpec as P
 
 BLOCK_PIX = 256
+
+
+def gather_by_bits(value, axis, dim):
+    ways, here, step = (lax.axis_size(axis), lax.axis_index(axis), value.shape[dim])
+    line, have = (value, 1)
+    while have < ways:
+        line = jnp.concatenate(
+            [line, lax.ppermute(line, axis, [(d, (d - have) % ways) for d in range(ways)])],
+            axis=dim,
+        )
+        have = 2 * have
+    return jnp.roll(line, here * step, axis=dim)
 
 
 def hamming(length):
@@ -58,7 +70,7 @@
     block_start = snap_index * local_pixel_blocks
     weighted = (snap_tiles.astype(jnp.float32) * beam_gain[:, None]).astype(jnp.bfloat16)
     own_map = lax.dynamic_slice_in_dim(tile_map, block_start, local_pixel_blocks, 1)
-    sky_cube = interpolate(lax.all_gather(weighted, "snap", axis=0, tiled=True), kernel, own_map)
+    sky_cube = interpolate(gather_by_bits(weighted, "snap", 0), kernel, own_map)
     cube_low = sky_cube.astype(jnp.bfloat16)
     per_group = 2
     turn_count = local_pixel_blocks // per_group

time: 278 us -> 269 us (0.968)
  waiting for transfers between devices: 55.4 us -> 41 us
  starting transfers between devices: 0.08 us -> 3.1 us
  other arithmetic: 143 us -> 146 us
    all_gather x1 -> x0, waiting for transfers between devices: 47.4 us -> none  [per_device(): lax.all_gather(weighted, 'snap', axis=0, tiled=True)]
    ppermute x0 -> x1, waiting for transfers between devices: none -> 31.9 us  [gather_by_bits(): lax.ppermute(line, axis, [(d, (d - have) % ways) for d in range(ways)])]
    all_gather x1 -> x0, local copies, waits for them, and re-layouts: 6.46 us -> none  [per_device(): lax.all_gather(weighted, 'snap', axis=0, tiled=True)]
    dynamic_slice x0 -> x1, local copies, waits for them, and re-layouts: none -> 4.58 us  [gather_by_bits(): return jnp.roll(line, here * step, axis=dim)]
    ppermute x0 -> x1, starting transfers between devices: none -> 3.06 us  [gather_by_bits(): lax.ppermute(line, axis, [(d, (d - have) % ways) for d in range(ways)])]
  transfers between devices with their start and end apart: 2 -> 2, of which waited for: 2 -> 2; matrix products, arithmetic and copies ran while one was open for 0% -> 1% of each run, Pallas kernels for 0% -> 0%
where the time goes in v1:
time: 269 us; the launch traced here: 268 us
  other arithmetic  146 us (54%)
  waiting for transfers between devices  41 us (15%)
  matrix products  29.4 us (11%)
  local copies, waits for them, and re-layouts  19 us (7%)
  blocking collectives  14.9 us (6%)
  between operations  14.1 us (5%)
  starting transfers between devices  3.1 us (1%)
    another operation x8, other arithmetic  137 us
    ppermute x1, waiting for transfers between devices, gather_by_bits(): lax.ppermute(line, axis, [(d, (d - have) % ways) for d in range(ways)])  31.9 us
    dot_general x8, matrix products, add_group(): jnp.einsum('woj,wjh->oh', partial_sky_cube, phasor_lookup, preferred_elem...  18 us
    all_to_all x1, blocking collectives, per_device(): lax.all_to_all(spread, 'chan', split_axis=3, concat_axis=1, tiled=True)  14.9 us
    reduce_scatter x1, waiting for transfers between devices, per_device(): lax.psum_scatter(regrouped, 'snap', scatter_dimension=2, tiled=True)  9.01 us
    dot_general x1, matrix products, interpolate(): jnp.einsum('scbt,sbtp->bcp', gathered_rows, kernels, preferred_element_ty...  7.02 us
    slice x8, local copies, waits for them, and re-layouts, phasor(): positions[0][:, None] * spatial[0][None, :]  6.87 us
  transfers between devices with their start and end apart: 2, of which 2 were waited for; matrix products, arithmetic and copies ran while one was open for 1% of the time, Pallas kernels for 0%

profile of v1, /device:TPU:0, one launch (start us, length us, event | category | flops | bytes accessed | tf_op | source)
XLA Modules:
  0.0 267.8 jit_solution(1228303697575822609)
XLA Ops:
  7.2 1.9 multiply_convert_fusion
  9.1 3.1 %collective-permute-start = (bf16[8,12,64,128]{3,2,1,0:T(8,128)(2,1)S(1)}, bf16[8,12,64,128]{3,2,1,0:T(8,128)(2,1)S(1)}, u32[]{:S(2)}, u32[]{:S(2)}) collective-permute-start(bf16[8,12,64,128]{3,2,1,0:T(8,128)(2,1)S(1)} %multiply_convert_fusion), channel_id=1, source_target_pairs={{0,16},{16,0},{1,17},{17,1},{2,18},{18,2},{3,19},{19,3},{4,20},{20... | collective-permute-start | bytes 4718600 | tf_op jit(solution)/shard_map/ppermute | solution.py:15
  12.2 0.8 bitcast_or_fusion
  13.1 0.8 compare_and_fusion
  13.9 0.7 convert_element_type.39
  14.7 31.9 %collective-permute-done = bf16[8,12,64,128]{3,2,1,0:T(8,128)(2,1)S(1)} collective-permute-done((bf16[8,12,64,128]{3,2,1,0:T(8,128)(2,1)S(1)}, bf16[8,12,64,128]{3,2,1,0:T(8,128)(2,1)S(1)}, u32[]{:S(2)}, u32[]{:S(2)}) %collective-permute-start) | collective-permute-done | bytes 1572896 | tf_op jit(solution)/shard_map/ppermute | solution.py:15
  46.6 2.1 fusion.11
  48.8 4.6 %copy.39 = bf16[16,12,64,128]{3,1,2,0:T(8,128)(2,1)} copy(bf16[16,12,64,128]{3,2,1,0:T(8,128)(2,1)S(1)} %fusion.11) | data formatting | bytes 6291456 | tf_op jit(solution)/shard_map/jit(_roll_dynamic)/dynamic_slice | solution.py:19
  53.3 3.4 %gather_fusion = bf16[256,12,128]{2,1,0:T(8,128)(2,1)S(1)} fusion(bf16[16,12,64,128]{3,1,2,0:T(8,128)(2,1)} %copy.39, s32[256]{0:T(256)S(1)} %reshape.93), kind=kCustom, calls=%fused_computation | custom fusion | bytes 1574912 | tf_op jit(solution)/shard_map/vmap(jit(_take))/gather | solution.py:59
  56.8 7.0 %fusion.70 = (bf16[16,12,256]{2,1,0:T(8,128)(2,1)S(1)}, f32[16,12,256]{2,1,0:T(8,128)S(1)}) fusion(bf16[16,16,128,256]{3,2,1,0:T(8,128)(2,1)} %param.10, bf16[16,16,12,128]{3,2,1,0:T(8,128)(2,1)S(1)} %bitcast.60, pred[16,16]{0,1:T(8,128)(4,1)S(1)} %copy.38), kind=kOutput, calls=%fused_computation.81 | convolution fusion | flops 201768960 | bytes 17858816 | tf_op jit(solution)/shard_map/scbt,sbtp->bcp/dot_general | solution.py:61
  63.8 162.4 %while.16 = (s32[]{:T(128)}, f32[12,4096]{1,0:T(8,128)S(1)}, bf16[16,12,256]{2,1,0:T(8,128)(2,1)S(1)}, f32[2,4096]{1,0:T(2,128)}, f32[2,2048]{1,0:T(2,128)S(1)},...) while((s32[]{:T(128)}, f32[12,4096]{1,0:T(8,128)S(1)}, ...), condition=%wide.region_1.2_spmd.clone, body=%wide.region_0.1_spmd.clone.sunk | while | flops 66158604 | bytes 8933619 | solution.py:90
  63.8 0.9 dynamic-slice_reduce_fusion.3
  64.7 17.1 %cosine_convert_fusion.2 = (bf16[2,256,2048]{2,1,0:T(8,128)(2,1)S(1)}, bf16[2,256,2048]{2,1,0:T(8,128)(2,1)}) fusion(f32[2048]{0:T(1024)S(1)} %bitcast.58, f32[2,256]{1,0:T(2,128)S(1)} %mul.444, f32[2048]{0:T(1024)S(1)} %bitcast.57, f32[2,256]{1,0:T(2,128)S(1)} %mul.445), kind=kLoop, calls=%fused_computation.7.clone.1 | loop fusion | flops 7340032 | bytes 4214784 | tf_op jit(solution)/shard_map/convert
  81.8 2.3 fusion.78
  84.1 0.9 dynamic-slice_reduce_fusion.3
  85.0 17.1 %cosine_convert_fusion.2 = (bf16[2,256,2048]{2,1,0:T(8,128)(2,1)S(1)}, bf16[2,256,2048]{2,1,0:T(8,128)(2,1)}) fusion(f32[2048]{0:T(1024)S(1)} %bitcast.58, f32[2,256]{1,0:T(2,128)S(1)} %mul.444, f32[2048]{0:T(1024)S(1)} %bitcast.57, f32[2,256]{1,0:T(2,128)S(1)} %mul.445), kind=kLoop, calls=%fused_computation.7.clone.1 | loop fusion | flops 7340032 | bytes 4214784 | tf_op jit(solution)/shard_map/convert
  102.1 2.3 fusion.78
  104.4 0.9 dynamic-slice_reduce_fusion.3
  105.3 17.1 %cosine_convert_fusion.2 = (bf16[2,256,2048]{2,1,0:T(8,128)(2,1)S(1)}, bf16[2,256,2048]{2,1,0:T(8,128)(2,1)}) fusion(f32[2048]{0:T(1024)S(1)} %bitcast.58, f32[2,256]{1,0:T(2,128)S(1)} %mul.444, f32[2048]{0:T(1024)S(1)} %bitcast.57, f32[2,256]{1,0:T(2,128)S(1)} %mul.445), kind=kLoop, calls=%fused_computation.7.clone.1 | loop fusion | flops 7340032 | bytes 4214784 | tf_op jit(solution)/shard_map/convert
  122.4 2.3 fusion.78
  124.7 0.9 dynamic-slice_reduce_fusion.3
  125.6 17.1 %cosine_convert_fusion.2 = (bf16[2,256,2048]{2,1,0:T(8,128)(2,1)S(1)}, bf16[2,256,2048]{2,1,0:T(8,128)(2,1)}) fusion(f32[2048]{0:T(1024)S(1)} %bitcast.58, f32[2,256]{1,0:T(2,128)S(1)} %mul.444, f32[2048]{0:T(1024)S(1)} %bitcast.57, f32[2,256]{1,0:T(2,128)S(1)} %mul.445), kind=kLoop, calls=%fused_computation.7.clone.1 | loop fusion | flops 7340032 | bytes 4214784 | tf_op jit(solution)/shard_map/convert
  142.7 2.3 fusion.78
  145.0 0.9 dynamic-slice_reduce_fusion.3
  145.9 17.1 %cosine_convert_fusion.2 = (bf16[2,256,2048]{2,1,0:T(8,128)(2,1)S(1)}, bf16[2,256,2048]{2,1,0:T(8,128)(2,1)}) fusion(f32[2048]{0:T(1024)S(1)} %bitcast.58, f32[2,256]{1,0:T(2,128)S(1)} %mul.444, f32[2048]{0:T(1024)S(1)} %bitcast.57, f32[2,256]{1,0:T(2,128)S(1)} %mul.445), kind=kLoop, calls=%fused_computation.7.clone.1 | loop fusion | flops 7340032 | bytes 4214784 | tf_op jit(solution)/shard_map/convert
  163.1 2.3 fusion.78
  165.3 0.9 dynamic-slice_reduce_fusion.3
  166.2 17.1 %cosine_convert_fusion.2 = (bf16[2,256,2048]{2,1,0:T(8,128)(2,1)S(1)}, bf16[2,256,2048]{2,1,0:T(8,128)(2,1)}) fusion(f32[2048]{0:T(1024)S(1)} %bitcast.58, f32[2,256]{1,0:T(2,128)S(1)} %mul.444, f32[2048]{0:T(1024)S(1)} %bitcast.57, f32[2,256]{1,0:T(2,128)S(1)} %mul.445), kind=kLoop, calls=%fused_computation.7.clone.1 | loop fusion | flops 7340032 | bytes 4214784 | tf_op jit(solution)/shard_map/convert
  183.4 2.3 fusion.78
  185.6 0.9 dynamic-slice_reduce_fusion.3
  186.5 17.1 %cosine_convert_fusion.2 = (bf16[2,256,2048]{2,1,0:T(8,128)(2,1)S(1)}, bf16[2,256,2048]{2,1,0:T(8,128)(2,1)}) fusion(f32[2048]{0:T(1024)S(1)} %bitcast.58, f32[2,256]{1,0:T(2,128)S(1)} %mul.444, f32[2048]{0:T(1024)S(1)} %bitcast.57, f32[2,256]{1,0:T(2,128)S(1)} %mul.445), kind=kLoop, calls=%fused_computation.7.clone.1 | loop fusion | flops 7340032 | bytes 4214784 | tf_op jit(solution)/shard_map/convert
  203.7 2.3 fusion.78
  205.9 0.9 dynamic-slice_reduce_fusion.3
  206.8 17.1 %cosine_convert_fusion.2 = (bf16[2,256,2048]{2,1,0:T(8,128)(2,1)S(1)}, bf16[2,256,2048]{2,1,0:T(8,128)(2,1)}) fusion(f32[2048]{0:T(1024)S(1)} %bitcast.58, f32[2,256]{1,0:T(2,128)S(1)} %mul.444, f32[2048]{0:T(1024)S(1)} %bitcast.57, f32[2,256]{1,0:T(2,128)S(1)} %mul.445), kind=kLoop, calls=%fused_computation.7.clone.1 | loop fusion | flops 7340032 | bytes 4214784 | tf_op jit(solution)/shard_map/convert
  224.0 2.3 fusion.78
  226.9 0.4 reshape.118
  227.3 14.9 %all_to_all.18 = f32[16,1,3072]{2,1,0:T(1,128)S(1)} all-to-all(f32[16,1,3072]{2,1,0:T(1,128)S(1)} %reshape.118), channel_id=1, replica_groups=mesh['snap'=2,'chan'=16] {'chan'}, dimensions={0} | all-to-all | bytes 393216 | tf_op jit(solution)/shard_map/all_to_all | solution.py:97
  242.2 0.5 broadcast.119
  242.7 1.1 reduce.8
  244.1 1.0 copy.44
  245.2 0.8 copy.46
  246.0 9.0 %reduce-scatter.2.cloned.1.call-done = f32[2,192,1,1,64]{1,4,3,0,2:T(8,128)} async-done(((f32[2,192,2,1,64]{1,4,3,0,2:T(8,128)}), f32[2,192,1,1,64]{1,4,3,0,2:T(8,128)}) %reduce-scatter.2.cloned.1.call-update) | async-done | bytes 98320 | tf_op jit(solution)/shard_map/reduce_scatter | solution.py:98
  255.0 0.9 fusion.68
  255.9 1.1 fusion.28
  257.0 1.1 fusion.26
  258.1 1.1 fusion.16
  259.1 1.1 fusion.15
  260.2 0.7 maximum_multiply_fusion
  (34 shorter events, 1.6 us)
Async XLA Ops:
  7.2 247.8 %reduce-scatter.2.cloned.1.call-start = ((), (), s32[]{:S(2)}) async-start(), calls=%async_computation.2 | async-start | bytes 393216 | tf_op jit(solution)/shard_map/reduce_scatter | solution.py:98
  9.1 37.5 %collective-permute-start = (bf16[8,12,64,128]{3,2,1,0:T(8,128)(2,1)S(1)}, bf16[8,12,64,128]{3,2,1,0:T(8,128)(2,1)S(1)}, u32[]{:S(2)}, u32[]{:S(2)}) collective-permute-start(bf16[8,12,64,128]{3,2,1,0:T(8,128)(2,1)S(1)} %multiply_convert_fusion), channel_id=1, source_target_pairs={{0,16},{16,0},{1,17},{17,1},{2,18},{18,2},{3,19},{19,3},{4,20},{20... | collective-permute-start | bytes 4718600 | tf_op jit(solution)/shard_map/ppermute | solution.py:15
Sparse Core Ops, SparseCore 0:
  245.2 9.6 reduce-scatter.1
